TPU v7x, 512 devices: a whole 4x8x8 slice. The times are simulated.
512 devices in a mesh: expert: 32 (over y, z_hi), dp: 16 (over x, z_lo, core).
Axes of the slice: x: 4, y: 8, z: 8 (z_hi: 4, z_lo: 2; z = z_hi * 2 + z_lo), core: 2. Of those that a mesh axis runs over, the one named last changes fastest.
Arguments:
- tokens: bfloat16 [65536, 1024], P(('expert', 'dp')), may hold values from -6 to 6
- out_grad: bfloat16 [65536, 1024], P(('expert', 'dp')), may hold values from -6 to 6
- expert_ids: int32 [65536, 8], P(('expert', 'dp')), may hold values from 0 to 127, as said below
- gate_scores: int32 [65536, 8], P(('expert', 'dp')), may hold values from 1 to 16
- w_gate: bfloat16 [512, 256, 384], P(('expert', 'dp')), may hold values from -0.1875 to 0.1875
- w_up: bfloat16 [512, 256, 384], P(('expert', 'dp')), may hold values from -0.1875 to 0.1875
- w_down: bfloat16 [512, 256, 384], P(('expert', 'dp')), may hold values from -0.3125 to 0.3125
Outputs:
- d_tokens: bfloat16 [65536, 1024], P(('expert', 'dp'))
- grad_gate: float32 [512, 256, 384], P(('expert', 'dp'))
- grad_up: float32 [512, 256, 384], P(('expert', 'dp'))
- grad_down: float32 [512, 256, 384], P(('expert', 'dp'))
Inputs may be any that keep to these rules, and one draw needn't show every extreme that they name: `expert_ids`: each token names 8 different experts. Among one device's 128 tokens every expert is named by exactly 8 of them.
All inputs are finite; a program needn't handle non-finite values.
Results may differ from a plain program's by a relative error of at most 0.007.
Values may be sent and summed in bfloat16 or wider, within the bound.
A program may use at most 64 MiB of HBM per device.

v0:
```python
import jax
import jax.numpy as jnp
from jax import lax
from jax.sharding import PartitionSpec as P


def partner_2(value, axis, stride):
    mask = 2**stride
    pairs = [(source, source ^ mask) for source in range(lax.axis_size(axis))]
    return lax.ppermute(value, axis, pairs)


def expert_pass(rows_in, grads_in, gates_in, gate_full, up_full, down_full):
    gate_pre = jnp.dot(rows_in, gate_full, preferred_element_type=jnp.float32)
    up_pre = jnp.dot(rows_in, up_full, preferred_element_type=jnp.float32)
    sigmoid_gate = jax.nn.sigmoid(gate_pre)
    silu_gate = gate_pre * sigmoid_gate
    hidden = (silu_gate * up_pre).astype(jnp.bfloat16)
    scaled = (gates_in.astype(jnp.float32)[:, None] * grads_in.astype(jnp.float32)).astype(
        jnp.bfloat16
    )
    grad_down = jnp.dot(scaled.T, hidden, preferred_element_type=jnp.float32)
    back_hidden = jnp.dot(scaled, down_full, preferred_element_type=jnp.float32)
    gate_back = (
        back_hidden * up_pre * sigmoid_gate * (1.0 + gate_pre * (1.0 - sigmoid_gate))
    ).astype(jnp.bfloat16)
    up_back = (back_hidden * silu_gate).astype(jnp.bfloat16)
    grad_gate = jnp.dot(rows_in.T, gate_back, preferred_element_type=jnp.float32)
    grad_up = jnp.dot(rows_in.T, up_back, preferred_element_type=jnp.float32)
    token_part = (
        jnp.dot(gate_back, gate_full.T, preferred_element_type=jnp.float32)
        + jnp.dot(up_back, up_full.T, preferred_element_type=jnp.float32)
    ).astype(jnp.bfloat16)
    return (grad_gate, grad_up, grad_down, token_part)


def gather_panels(panels_all, dp_index):
    for bit_pos in (0, 1):
        partner = partner_2(panels_all, "dp", bit_pos)
        high_side = dp_index >> bit_pos & 1 == 1
        panels_all = jnp.where(
            high_side,
            jnp.concatenate((partner, panels_all), axis=1),
            jnp.concatenate((panels_all, partner), axis=1),
        )
    return panels_all


def per_device(tokens, out_grad, expert_ids, gate_scores, w_gate, w_up, w_down):
    tok_dev, top_k = expert_ids.shape
    model_width = tokens.shape[1]
    cycle_size = lax.axis_size("expert")
    data_size = lax.axis_size("dp")
    experts = cycle_size * data_size // 4
    capacity = tok_dev * top_k // experts
    per_replica = capacity // 4
    slot_count = experts * capacity
    routed = tok_dev * top_k
    flat_ids = expert_ids.reshape(routed)
    route_iota = jnp.arange(routed, dtype=jnp.int32)
    matches = (flat_ids[:, None] == jnp.arange(experts, dtype=jnp.int32)[None, :]).astype(
        jnp.bfloat16
    )
    earlier_mask = (route_iota[:, None] > route_iota[None, :]).astype(jnp.bfloat16)
    earlier_count = jnp.dot(earlier_mask, matches, preferred_element_type=jnp.float32)
    before_rank = jnp.sum(earlier_count * matches.astype(jnp.float32), axis=1).astype(jnp.int32)
    target = flat_ids * capacity + before_rank
    placed = (jnp.arange(slot_count, dtype=jnp.int32)[:, None] == target[None, :]).astype(
        jnp.bfloat16
    )
    scores = gate_scores.astype(jnp.float32)
    gate_weight = (scores / jnp.sum(scores, axis=1, keepdims=True)).astype(jnp.bfloat16)
    slot_gate = jnp.dot(placed, gate_weight.reshape(routed), preferred_element_type=jnp.float32)
    slot_gate = slot_gate.astype(jnp.bfloat16).reshape(cycle_size, data_size, per_replica)
    selection = (
        (route_iota // top_k)[:, None] == jnp.arange(tok_dev, dtype=jnp.int32)[None, :]
    ).astype(jnp.bfloat16)
    picker = jnp.dot(placed, selection, preferred_element_type=jnp.float32).astype(jnp.bfloat16)
    sent_tokens = jnp.dot(picker, tokens, preferred_element_type=jnp.float32).astype(jnp.bfloat16)
    sent_grads = jnp.dot(picker, out_grad, preferred_element_type=jnp.float32).astype(jnp.bfloat16)
    sent_tokens = sent_tokens.reshape(cycle_size, data_size, per_replica, model_width)
    sent_grads = sent_grads.reshape(cycle_size, data_size, per_replica, model_width)
    got_tokens, got_grads, got_gates = (
        lax.all_to_all(
            lax.all_to_all(sent_tokens, "expert", split_axis=0, concat_axis=0, tiled=True),
            "dp",
            split_axis=1,
            concat_axis=1,
            tiled=True,
        ),
        lax.all_to_all(
            lax.all_to_all(sent_grads, "expert", split_axis=0, concat_axis=0, tiled=True),
            "dp",
            split_axis=1,
            concat_axis=1,
            tiled=True,
        ),
        lax.all_to_all(
            lax.all_to_all(slot_gate, "expert", split_axis=0, concat_axis=0, tiled=True),
            "dp",
            split_axis=1,
            concat_axis=1,
            tiled=True,
        ),
    )
    row_count = cycle_size * data_size * per_replica
    dp_index = lax.axis_index("dp")
    panels_all = gather_panels(jnp.concatenate((w_gate, w_up, w_down), axis=0), dp_index)
    grad_gate, grad_up, grad_down, token_part = expert_pass(
        got_tokens.reshape(row_count, model_width),
        got_grads.reshape(row_count, model_width),
        got_gates.reshape(row_count),
        panels_all[0],
        panels_all[1],
        panels_all[2],
    )
    returned = token_part.reshape(cycle_size, data_size, per_replica, model_width)
    returned = lax.all_to_all(
        lax.all_to_all(returned, "expert", split_axis=0, concat_axis=0, tiled=True),
        "dp",
        split_axis=1,
        concat_axis=1,
        tiled=True,
    )
    d_tokens = jnp.dot(
        picker.T, returned.reshape(slot_count, model_width), preferred_element_type=jnp.float32
    )
    d_tokens = d_tokens.astype(jnp.bfloat16)
    quarter = w_gate.shape[1]
    hidden_size = w_gate.shape[2]
    grad_stack = jnp.stack((grad_gate, grad_up, grad_down)).reshape(3, 2, 2, quarter, hidden_size)
    bit_order = (0, 1)
    for bit_pos in bit_order:
        axis_pos = 2 if bit_pos == 0 else 1
        high_side = dp_index >> bit_pos & 1
        kept_part = lax.dynamic_index_in_dim(grad_stack, high_side, axis_pos, keepdims=True)
        sent_part = lax.dynamic_index_in_dim(grad_stack, 1 - high_side, axis_pos, keepdims=True)
        grad_stack = kept_part + partner_2(sent_part, "dp", bit_pos)
    grad_stack = grad_stack.reshape(3, quarter, hidden_size)
    return (d_tokens, grad_stack[0:1], grad_stack[1:2], grad_stack[2:3])


def solution(mesh):
    placed = (
        P(("expert", "dp"), None),
        P(("expert", "dp"), None),
        P(("expert", "dp"), None),
        P(("expert", "dp"), None),
        P(("expert", "dp"), None, None),
        P(("expert", "dp"), None, None),
        P(("expert", "dp"), None, None),
    )
    return jax.shard_map(
        per_device,
        mesh=mesh,
        in_specs=placed,
        out_specs=(
            P(("expert", "dp"), None),
            P(("expert", "dp"), None, None),
            P(("expert", "dp"), None, None),
            P(("expert", "dp"), None, None),
        ),
        check_vma=False,
    )
```

profile of v0, /device:TPU:24, one launch (start us, length us, event | category | flops | bytes accessed | tf_op | source)
XLA Modules:
  0.0 454.0 jit_solution(835749584466923361)
XLA Ops:
  4.4 15.9 %all-to-all-start = ((bf16[32,16,2]{1,2,0:T(2,128)(2,1)}), bf16[32,16,2]{1,2,0:T(2,128)(2,1)S(1)}, u32[]{:S(2)}, u32[]{:S(2)}) async-start(bf16[32,16,2]{1,2,0:T(2,128)(2,1)} %copy.58), calls=%async_computation | async-start | bytes 32768 | tf_op jit(solution)/shard_map/all_to_all | solution.py:99
  21.3 8.2 %all-to-all-done = bf16[32,16,2]{1,2,0:T(2,128)(2,1)S(1)} async-done(((bf16[32,16,2]{1,2,0:T(2,128)(2,1)}), bf16[32,16,2]{1,2,0:T(2,128)(2,1)S(1)}, u32[]{:S(2)}, u32[]{:S(2)}) %all-to-all-start) | async-done | bytes 2080 | tf_op jit(solution)/shard_map/all_to_all | solution.py:99
  30.2 5.3 %all-to-all-start.1 = ((bf16[32,16,2]{0,2,1:T(2,128)(2,1)}), bf16[32,16,2]{0,2,1:T(2,128)(2,1)S(1)}, u32[]{:S(2)}, u32[]{:S(2)}) async-start(bf16[32,16,2]{0,2,1:T(2,128)(2,1)} %copy.59), calls=%async_computation.1 | async-start | bytes 16384 | tf_op jit(solution)/shard_map/all_to_all | solution.py:98
  41.5 7.6 %all-to-all-start.4 = ((bf16[32,16,2,1024]{3,2,1,0:T(2,128)(2,1)}), bf16[32,16,2,1024]{3,2,1,0:T(2,128)(2,1)}, u32[]{:S(2)}, u32[]{:S(2)}) async-start(bf16[32,16,2,1024]{3,2,1,0:T(2,128)(2,1)} %reshape.104), calls=%async_computation.4 | async-start | bytes 4194304 | tf_op jit(solution)/shard_map/all_to_all | solution.py:85
  52.1 54.4 %all-to-all-done.4 = bf16[32,16,2,1024]{3,2,1,0:T(2,128)(2,1)} async-done(((bf16[32,16,2,1024]{3,2,1,0:T(2,128)(2,1)}), bf16[32,16,2,1024]{3,2,1,0:T(2,128)(2,1)}, u32[]{:S(2)}, u32[]{:S(2)}) %all-to-all-start.4) | async-done | bytes 2097184 | tf_op jit(solution)/shard_map/all_to_all | solution.py:85
  106.5 12.6 %all-to-all-start.2 = ((bf16[32,16,2,1024]{3,2,1,0:T(2,128)(2,1)}), bf16[32,16,2,1024]{3,2,1,0:T(2,128)(2,1)S(1)}, u32[]{:S(2)}, u32[]{:S(2)}) async-start(bf16[32,16,2,1024]{3,2,1,0:T(2,128)(2,1)} %reshape.103), calls=%async_computation.2 | async-start | bytes 4194304 | tf_op jit(solution)/shard_map/all_to_all | solution.py:92
  119.1 4.9 %copy.65 = bf16[32,16,2,1024]{3,2,0,1:T(2,128)(2,1)} copy(bf16[32,16,2,1024]{3,2,1,0:T(2,128)(2,1)} %all-to-all-done.4) | data formatting | bytes 4194304 | tf_op jit(solution)/shard_map/all_to_all | solution.py:85
  124.0 46.8 %all-to-all-done.2 = bf16[32,16,2,1024]{3,2,1,0:T(2,128)(2,1)S(1)} async-done(((bf16[32,16,2,1024]{3,2,1,0:T(2,128)(2,1)}), bf16[32,16,2,1024]{3,2,1,0:T(2,128)(2,1)S(1)}, u32[]{:S(2)}, u32[]{:S(2)}) %all-to-all-start.2) | async-done | bytes 2097184 | tf_op jit(solution)/shard_map/all_to_all | solution.py:92
  172.1 4.0 all-to-all-start.5
  176.1 4.9 %copy.62 = bf16[32,16,2,1024]{3,2,0,1:T(2,128)(2,1)} copy(bf16[32,16,2,1024]{3,2,1,0:T(2,128)(2,1)} %copy-done.7) | data formatting | bytes 4194304 | tf_op jit(solution)/shard_map/all_to_all | solution.py:92
  181.0 23.0 %all-to-all-done.5 = bf16[32,16,2,1024]{3,2,0,1:T(2,128)(2,1)S(1)} async-done(((bf16[32,16,2,1024]{3,2,0,1:T(2,128)(2,1)}), bf16[32,16,2,1024]{3,2,0,1:T(2,128)(2,1)S(1)}, u32[]{:S(2)}, u32[]{:S(2)}) %all-to-all-start.5) | async-done | bytes 2097184 | tf_op jit(solution)/shard_map/all_to_all | solution.py:84
  205.3 3.7 all-to-all-start.3
  215.2 3.7 collective-permute-start.1
  219.0 42.1 %collective-permute-done.1 = bf16[3,512,384]{2,1,0:T(8,128)(2,1)} collective-permute-done((bf16[3,512,384]{2,1,0:T(8,128)(2,1)S(1)}, bf16[3,512,384]{2,1,0:T(8,128)(2,1)}, u32[]{:S(2)}, u32[]{:S(2)}) %collective-permute-start.1) | collective-permute-done | bytes 1179680 | tf_op jit(solution)/shard_map/ppermute | solution.py:10
  261.1 3.6 maximum_select_fusion
  264.7 3.6 copy.66
  268.3 4.3 reshape.105
  272.6 4.3 fusion.17
  286.6 4.1 convert_element_type.90
  290.8 4.6 %multiply_convert_fusion.4 = (bf16[1024,384]{1,0:T(8,128)(2,1)S(1)}, bf16[1024,384]{1,0:T(8,128)(2,1)S(1)}) fusion(f32[1024,384]{1,0:T(8,128)} %fusion.17, f32[1024,384]{1,0:T(8,128)} %fusion.16, bf16[1024,1024]{1,0:T(8,128)(2,1)} %convert_element_type.90, bf16[3,1024,384]{2,1,0:T(8,128)(2,1)} %maximum_select_fusion), kind=kOutput, calls=%fused_computation.19 | convolution fusion | flops 810418176 | bytes 7602176 | tf_op jit(solution)/shard_map/dot_general | solution.py:23
  299.4 4.1 reshape.106
  303.5 16.3 %all-to-all-start.6 = ((bf16[32,16,2,1024]{3,2,1,0:T(2,128)(2,1)}), bf16[32,16,2,1024]{3,2,1,0:T(2,128)(2,1)}, u32[]{:S(2)}, u32[]{:S(2)}) async-start(bf16[32,16,2,1024]{3,2,1,0:T(2,128)(2,1)} %reshape.106), calls=%async_computation.6 | async-start | bytes 4194304 | tf_op jit(solution)/shard_map/all_to_all | solution.py:119
  322.6 5.3 %copy.71 = f32[32,16,2,1024]{3,2,1,0:T(2,128)} copy(f32[32,16,2,1024]{3,1,2,0:T(8,128)S(1)} %copy_convert_fusion) | data formatting | bytes 8388608 | tf_op jit(solution)/shard_map/convert_element_type | solution.py:19
  328.0 6.1 %reshape.111 = f32[1024,1024]{1,0:T(8,128)} reshape(f32[32,16,2,1024]{3,2,1,0:T(2,128)} %copy.71) | data formatting | bytes 8388608 | tf_op jit(solution)/shard_map/convert_element_type | solution.py:19
  334.0 3.9 fusion.3
  337.9 4.1 copy.76
  355.6 19.4 %all-to-all-done.6 = bf16[32,16,2,1024]{3,2,1,0:T(2,128)(2,1)} async-done(((bf16[32,16,2,1024]{3,2,1,0:T(2,128)(2,1)}), bf16[32,16,2,1024]{3,2,1,0:T(2,128)(2,1)}, u32[]{:S(2)}, u32[]{:S(2)}) %all-to-all-start.6) | async-done | bytes 2097184 | tf_op jit(solution)/shard_map/all_to_all | solution.py:119
  375.0 4.8 %copy.67 = bf16[32,16,2,1024]{3,2,0,1:T(2,128)(2,1)} copy(bf16[32,16,2,1024]{3,2,1,0:T(2,128)(2,1)} %all-to-all-done.6) | data formatting | bytes 4194304 | tf_op jit(solution)/shard_map/all_to_all | solution.py:119
  379.8 10.0 %all-to-all-start.7 = ((bf16[32,16,2,1024]{3,2,0,1:T(2,128)(2,1)}), bf16[32,16,2,1024]{3,2,0,1:T(2,128)(2,1)}, u32[]{:S(2)}, u32[]{:S(2)}) async-start(bf16[32,16,2,1024]{3,2,0,1:T(2,128)(2,1)} %copy.67), calls=%async_computation.7 | async-start | bytes 4194304 | tf_op jit(solution)/shard_map/all_to_all | solution.py:118
  393.6 3.8 collective-permute-start.3
  397.4 44.6 %collective-permute-done.3 = f32[3,1,1,256,384]{4,3,2,1,0:T(8,128)} collective-permute-done((f32[3,1,1,256,384]{4,3,2,1,0:T(8,128)}, f32[3,1,1,256,384]{4,3,2,1,0:T(8,128)}, u32[]{:S(2)}, u32[]{:S(2)}) %collective-permute-start.3) | collective-permute-done | bytes 1179680 | tf_op jit(solution)/shard_map/ppermute | solution.py:10
  444.4 5.1 %copy.68 = bf16[32,16,2,1024]{3,2,1,0:T(2,128)(2,1)} copy(bf16[32,16,2,1024]{3,2,0,1:T(2,128)(2,1)} %all-to-all-done.7) | data formatting | bytes 4194304 | tf_op jit(solution)/shard_map/all_to_all | solution.py:118
  (101 shorter events, 63.3 us)
Async XLA Ops:
  0.6 34.9 %copy-start = (bf16[128,1024]{1,0:T(8,128)(2,1)S(1)}, bf16[128,1024]{1,0:T(8,128)(2,1)}, u32[]{:S(2)}) copy-start(bf16[128,1024]{1,0:T(8,128)(2,1)} %param.7) | copy-start | bytes 786436
  4.4 25.1 %all-to-all-start = ((bf16[32,16,2]{1,2,0:T(2,128)(2,1)}), bf16[32,16,2]{1,2,0:T(2,128)(2,1)S(1)}, u32[]{:S(2)}, u32[]{:S(2)}) async-start(bf16[32,16,2]{1,2,0:T(2,128)(2,1)} %copy.58), calls=%async_computation | async-start | bytes 32768 | tf_op jit(solution)/shard_map/all_to_all | solution.py:99
  21.3 27.8 %copy-start.9 = (bf16[1024,128]{1,0:T(8,128)(2,1)}, bf16[1024,128]{1,0:T(8,128)(2,1)S(1)}, u32[]{:S(2)}) copy-start(bf16[1024,128]{1,0:T(8,128)(2,1)S(1)} %fusion.8) | copy-start | bytes 786436
  30.2 11.3 %all-to-all-start.1 = ((bf16[32,16,2]{0,2,1:T(2,128)(2,1)}), bf16[32,16,2]{0,2,1:T(2,128)(2,1)S(1)}, u32[]{:S(2)}, u32[]{:S(2)}) async-start(bf16[32,16,2]{0,2,1:T(2,128)(2,1)} %copy.59), calls=%async_computation.1 | async-start | bytes 16384 | tf_op jit(solution)/shard_map/all_to_all | solution.py:98
  38.5 10.6 %copy-start.16 = (bf16[128,1024]{1,0:T(8,128)(2,1)S(1)}, bf16[128,1024]{1,0:T(8,128)(2,1)}, u32[]{:S(2)}) copy-start(bf16[128,1024]{1,0:T(8,128)(2,1)} %param.8) | copy-start | bytes 786436
  41.5 8.3 %copy-start.20 = (bf16[32,16,2]{0,2,1:T(2,128)(2,1)}, bf16[32,16,2]{0,2,1:T(2,128)(2,1)S(1)}, u32[]{:S(2)}) copy-start(bf16[32,16,2]{0,2,1:T(2,128)(2,1)S(1)} %all-to-all-done.1) | copy-start | bytes 6148
  41.5 65.0 %all-to-all-start.4 = ((bf16[32,16,2,1024]{3,2,1,0:T(2,128)(2,1)}), bf16[32,16,2,1024]{3,2,1,0:T(2,128)(2,1)}, u32[]{:S(2)}, u32[]{:S(2)}) async-start(bf16[32,16,2,1024]{3,2,1,0:T(2,128)(2,1)} %reshape.104), calls=%async_computation.4 | async-start | bytes 4194304 | tf_op jit(solution)/shard_map/all_to_all | solution.py:85
  106.5 64.2 %all-to-all-start.2 = ((bf16[32,16,2,1024]{3,2,1,0:T(2,128)(2,1)}), bf16[32,16,2,1024]{3,2,1,0:T(2,128)(2,1)S(1)}, u32[]{:S(2)}, u32[]{:S(2)}) async-start(bf16[32,16,2,1024]{3,2,1,0:T(2,128)(2,1)} %reshape.103), calls=%async_computation.2 | async-start | bytes 4194304 | tf_op jit(solution)/shard_map/all_to_all | solution.py:92
  172.1 31.9 %all-to-all-start.5 = ((bf16[32,16,2,1024]{3,2,0,1:T(2,128)(2,1)}), bf16[32,16,2,1024]{3,2,0,1:T(2,128)(2,1)S(1)}, u32[]{:S(2)}, u32[]{:S(2)}) async-start(bf16[32,16,2,1024]{3,2,0,1:T(2,128)(2,1)} %copy.65), calls=%async_computation.5 | async-start | bytes 4194304 | tf_op jit(solution)/shard_map/all_to_all | solution.py:84
  181.0 28.1 %copy-start.17 = (bf16[1,256,384]{2,1,0:T(8,128)(2,1)S(1)}, bf16[1,256,384]{2,1,0:T(8,128)(2,1)}, u32[]{:S(2)}) copy-start(bf16[1,256,384]{2,1,0:T(8,128)(2,1)} %param.11) | copy-start | bytes 589828
  181.0 28.1 %copy-start.18 = (bf16[1,256,384]{2,1,0:T(8,128)(2,1)S(1)}, bf16[1,256,384]{2,1,0:T(8,128)(2,1)}, u32[]{:S(2)}) copy-start(bf16[1,256,384]{2,1,0:T(8,128)(2,1)} %param.12) | copy-start | bytes 589828
  181.0 28.2 %copy-start.19 = (bf16[1,256,384]{2,1,0:T(8,128)(2,1)S(1)}, bf16[1,256,384]{2,1,0:T(8,128)(2,1)}, u32[]{:S(2)}) copy-start(bf16[1,256,384]{2,1,0:T(8,128)(2,1)} %param.13) | copy-start | bytes 589828
  205.3 75.2 %all-to-all-start.3 = ((bf16[32,16,2,1024]{3,2,0,1:T(2,128)(2,1)}), bf16[32,16,2,1024]{3,2,0,1:T(2,128)(2,1)S(1)}, u32[]{:S(2)}, u32[]{:S(2)}) async-start(bf16[32,16,2,1024]{3,2,0,1:T(2,128)(2,1)} %copy.62), calls=%async_computation.3 | async-start | bytes 4194304 | tf_op jit(solution)/shard_map/all_to_all | solution.py:91
  209.1 9.9 %copy-start.21 = (bf16[32,16,2]{0,2,1:T(2,128)(2,1)S(1)}, bf16[32,16,2]{0,2,1:T(2,128)(2,1)}, u32[]{:S(2)}) copy-start(bf16[32,16,2]{0,2,1:T(2,128)(2,1)} %copy-done.20) | copy-start | bytes 6148
  209.2 2.2 copy-start.13
  209.2 4.0 collective-permute-start
  215.2 45.9 %collective-permute-start.1 = (bf16[3,512,384]{2,1,0:T(8,128)(2,1)S(1)}, bf16[3,512,384]{2,1,0:T(8,128)(2,1)}, u32[]{:S(2)}, u32[]{:S(2)}) collective-permute-start(bf16[3,512,384]{2,1,0:T(8,128)(2,1)S(1)} %maximum_select_fusion.1), channel_id=1, source_target_pairs={{0,2},{1,3},{2,0},{3,1},{4,6},{5,7},{6,4},{7,5},{8,10},{9,11},{10,... | collective-permute-start | bytes 3538952 | tf_op jit(solution)/shard_map/ppermute | solution.py:10
  219.0 45.7 %copy-start.4 = (bf16[32,16,2,1024]{3,2,0,1:T(2,128)(2,1)S(1)}, bf16[32,16,2,1024]{3,2,0,1:T(2,128)(2,1)}, u32[]{:S(2)}) copy-start(bf16[32,16,2,1024]{3,2,0,1:T(2,128)(2,1)} %copy-done.3) | copy-start | bytes 6291460
  272.6 4.3 copy-start.5
  290.8 4.6 %copy-start.8 = (bf16[3,1024,384]{2,1,0:T(8,128)(2,1)S(1)}, bf16[3,1024,384]{2,1,0:T(8,128)(2,1)}, u32[]{:S(2)}) copy-start(bf16[3,1024,384]{2,1,0:T(8,128)(2,1)} %maximum_select_fusion) | copy-start | bytes 7077892
  303.5 71.5 %all-to-all-start.6 = ((bf16[32,16,2,1024]{3,2,1,0:T(2,128)(2,1)}), bf16[32,16,2,1024]{3,2,1,0:T(2,128)(2,1)}, u32[]{:S(2)}, u32[]{:S(2)}) async-start(bf16[32,16,2,1024]{3,2,1,0:T(2,128)(2,1)} %reshape.106), calls=%async_computation.6 | async-start | bytes 4194304 | tf_op jit(solution)/shard_map/all_to_all | solution.py:119
  337.9 4.1 copy-start.6
  344.6 3.0 copy-start.12
  344.6 3.0 copy-start.15
  344.6 4.3 copy-start.24
  347.6 2.0 copy-start.23
  351.3 2.1 copy-start.2
  353.4 36.4 %collective-permute-start.2 = (f32[3,2,1,256,384]{4,3,2,1,0:T(8,128)S(1)}, f32[3,2,1,256,384]{4,3,2,1,0:T(8,128)}, u32[]{:S(2)}, u32[]{:S(2)}) collective-permute-start(f32[3,2,1,256,384]{4,3,2,1,0:T(8,128)S(1)} %constant_dynamic-slice_fusion.1), channel_id=1, source_target_pairs={{0,1},{1,0},{2,3},{3,2},{4,5},{5,4},{6,7},{7,6},{8,9},{9,8},{10,11... | collective-permute-start | bytes 7077896 | tf_op jit(solution)/shard_map/ppermute | solution.py:10
  379.8 64.6 %all-to-all-start.7 = ((bf16[32,16,2,1024]{3,2,0,1:T(2,128)(2,1)}), bf16[32,16,2,1024]{3,2,0,1:T(2,128)(2,1)}, u32[]{:S(2)}, u32[]{:S(2)}) async-start(bf16[32,16,2,1024]{3,2,0,1:T(2,128)(2,1)} %copy.67), calls=%async_computation.7 | async-start | bytes 4194304 | tf_op jit(solution)/shard_map/all_to_all | solution.py:118
  393.6 48.3 %collective-permute-start.3 = (f32[3,1,1,256,384]{4,3,2,1,0:T(8,128)}, f32[3,1,1,256,384]{4,3,2,1,0:T(8,128)}, u32[]{:S(2)}, u32[]{:S(2)}) collective-permute-start(f32[3,1,1,256,384]{4,3,2,1,0:T(8,128)} %constant_dynamic-slice_fusion), channel_id=1, source_target_pairs={{0,2},{1,3},{2,0},{3,1},{4,6},{5,7},{6,4},{7,5},{8,10},{9,11},{10,... | collective-permute-start | bytes 3538952 | tf_op jit(solution)/shard_map/ppermute | solution.py:10
  449.5 2.8 copy-start.10
  449.5 4.0 copy-start.1
  (5 other events, 7.2 us)
where the time goes:
time: 463 us; the launch traced here: 454 us
  waiting for transfers between devices  243 us (52%)
  starting transfers between devices  87.3 us (19%)
  local copies, waits for them, and re-layouts  76.2 us (16%)
  matrix products  26.8 us (6%)
  other arithmetic  18.9 us (4%)
    ppermute x4, waiting for transfers between devices, partner_2(): return lax.ppermute(value, axis, pairs)  88.4 us
    all_to_all x1, waiting for transfers between devices, per_device(): lax.all_to_all(sent_tokens, 'expert', split_axis=0, concat_axis=0, tiled=...  54.4 us
    all_to_all x1, waiting for transfers between devices, per_device(): lax.all_to_all(sent_grads, 'expert', split_axis=0, concat_axis=0, tiled=T...  46.8 us
    all_to_all x1, waiting for transfers between devices, per_device(): lax.all_to_all(lax.all_to_all(sent_tokens, 'expert', split_axis=0, concat...  23 us
    all_to_all x1, waiting for transfers between devices, per_device(): lax.all_to_all(returned, 'expert', split_axis=0, concat_axis=0, tiled=True)  19.4 us
    all_to_all x1, starting transfers between devices, per_device(): lax.all_to_all(returned, 'expert', split_axis=0, concat_axis=0, tiled=True)  16.3 us
    all_to_all x1, starting transfers between devices, per_device(): lax.all_to_all(slot_gate, 'expert', split_axis=0, concat_axis=0, tiled=True)  15.9 us
    all_to_all x1, starting transfers between devices, per_device(): lax.all_to_all(sent_grads, 'expert', split_axis=0, concat_axis=0, tiled=T...  12.6 us
  transfers between devices with their start and end apart: 12, of which 9 were waited for; matrix products, arithmetic and copies ran while one was open for 18% of the time, Pallas kernels for 0%

commit v1 on v0

v1 whole, which is shorter than its diff:
```python
import jax
import jax.numpy as jnp
from jax import lax
from jax.experimental import pallas as pl
from jax.experimental.pallas import tpu as pltpu
from jax.sharding import PartitionSpec as P

MESH = pl.DeviceIdType.MESH
TOK = 128
D = 1024
HID = 384
EXPERTS = 128
ROWS = 1024
CHUNKS = 4
CHUNK = ROWS // CHUNKS
DQ = 256
F32 = jnp.float32
BF16 = jnp.bfloat16


def dot(lhs, rhs, contract):
    return lax.dot_general(lhs, rhs, (contract, ((), ())), preferred_element_type=F32)


def remote(src, dst, send_sem, recv_sem, device):
    return pltpu.make_async_remote_copy(
        src_ref=src, dst_ref=dst, send_sem=send_sem, recv_sem=recv_sem,
        device_id=device, device_id_type=MESH)


def device_at(x, y, z_pair, z_low, core):
    return {"expert": y * 4 + z_pair, "dp": x * 4 + z_low * 2 + core}


def dy_of(chunk, side):
    return jnp.where(side == 0, 4 - chunk, jnp.where(chunk == 0, 0, 4 + chunk))


def place_of(dy):
    return {4: (0, 0), 0: (0, 1), 3: (1, 0), 5: (1, 1), 2: (2, 0), 6: (2, 1), 1: (3, 0), 7: (3, 1)}[dy]


def slot_of(chunk, side, dx, j):
    return chunk * 32 + side * 16 + dx * 4 + j


def one_hot(condition):
    return jnp.where(condition, 1.0, 0.0)


def routing(id_blocks, expert_at, score_blocks, spread):
    each = EXPERTS // len(id_blocks)
    local = lax.broadcasted_iota(jnp.int32, (each, TOK), 0)
    experts = expert_at(local)
    members, gates = [], []
    for n, ids in enumerate(id_blocks):
        if score_blocks is not None:
            score = score_blocks[n].astype(F32)
            gate = (score / jnp.sum(score, axis=0, keepdims=True)).astype(BF16).astype(F32)
        member = jnp.zeros((each, TOK), F32)
        gate_of = jnp.zeros((each, TOK), F32)
        for k in range(8):
            hit = one_hot(experts == ids[k:k + 1, :])
            member = member + hit
            if score_blocks is not None:
                gate_of = gate_of + hit * gate[k:k + 1, :]
        members.append(member)
        gates.append(gate_of)
    member = jnp.concatenate(members, axis=0).astype(BF16)
    before = one_hot(lax.broadcasted_iota(jnp.int32, (TOK, TOK), 0)
                     < lax.broadcasted_iota(jnp.int32, (TOK, TOK), 1)).astype(BF16)
    rank = dot(member, before, ((1,), (0,)))
    wide_member = dot(spread, member, ((1,), (0,)))
    wide_rank = dot(spread, rank.astype(BF16), ((1,), (0,)))
    slot_rank = lax.rem(lax.broadcasted_iota(jnp.int32, (ROWS, TOK), 0), 8).astype(F32)
    chosen = jnp.where(wide_rank == slot_rank, wide_member, 0.0)
    if score_blocks is None:
        return chosen.astype(BF16), None
    wide_gate = dot(spread, jnp.concatenate(gates, axis=0).astype(BF16), ((1,), (0,)))
    return chosen.astype(BF16), (chosen * wide_gate).astype(BF16)


def body(tok_in, grad_in, ids_in, scores_in, wg, wu, wd, d_tok, g_gate, g_up, g_down,
         tok, grad, meta, spread, pick_y, pick_z, gated_z, ring_t, ring_i, gath_g, gath_m,
         send_t, send_g, recv_t, recv_g, part_y, part_z, ret_y, ret_z, sum_y, sum_z, got_y, got_z, weights, acc,
         half_s, half_r, quarter_s, quarter_r,
         load_sem, ring_send, ring_recv, gath_send, gath_recv, id_send, id_recv,
         send_sem, recv_t_sem, recv_g_sem, w_send, w_recv, ret_send, ret_y_sem, ret_z_sem,
         sum_send, got_y_sem, got_z_sem, red_send, red_recv):
    e_pos = lax.axis_index("expert")
    d_pos = lax.axis_index("dp")
    y, z_pair = e_pos // 4, lax.rem(e_pos, 4)
    x, part = d_pos // 4, lax.rem(d_pos, 4)
    z_low, core = part // 2, lax.rem(part, 2)
    other_core = device_at(x, y, z_pair, z_low, 1 - core)
    other_chip = device_at(x, y, z_pair, 1 - z_low, core)
    part_core = z_low * 2 + 1 - core
    part_chip = (1 - z_low) * 2 + core
    part_far = (1 - z_low) * 2 + 1 - core
    dz_near = jnp.where(z_low == 0, 1, 3)
    dz_back = 4 - dz_near
    y_next = device_at(x, lax.rem(y + 1, 8), z_pair, z_low, core)
    y_prev = device_at(x, lax.rem(y + 7, 8), z_pair, z_low, core)
    z_near = device_at(x, y, lax.rem(z_pair + dz_near, 4), z_low, core)
    z_back = device_at(x, y, lax.rem(z_pair + dz_back, 4), 1 - z_low, core)
    z_far = device_at(x, y, lax.rem(z_pair + 2, 4), 1 - z_low, core)

    def rows_of(p):
        return pl.ds(pl.multiple_of(p * DQ, DQ), DQ)

    z_from = device_at(x, y, lax.rem(z_pair + dz_back, 4), z_low, core)

    entry = pltpu.get_barrier_semaphore()

    def greet(target):
        pl.semaphore_signal(entry, inc=1, device_id=target, device_id_type=MESH)

    def greet_xy(index, carry):
        greet(device_at(lax.rem(x + lax.rem(index, 4), 4), lax.rem(y + index // 4, 8), z_pair, z_low, core))
        return carry

    def greet_xz(index, carry):
        x_to = lax.rem(x + index, 4)
        greet(device_at(x_to, y, lax.rem(z_pair + dz_near, 4), z_low, core))
        greet(device_at(x_to, y, lax.rem(z_pair + dz_back, 4), z_low, core))
        greet(device_at(x_to, y, lax.rem(z_pair + dz_back, 4), 1 - z_low, core))
        greet(device_at(x_to, y, lax.rem(z_pair + 2, 4), 1 - z_low, core))
        return carry

    greet(other_core)
    greet(other_chip)
    lax.fori_loop(0, 4, greet_xz, 0)
    lax.fori_loop(1, 32, greet_xy, 0)

    own_weights = weights.at[:, rows_of(part)]
    loads = [pltpu.make_async_copy(grad_in, grad, load_sem.at[0]),
             pltpu.make_async_copy(tok_in, tok, load_sem.at[1]),
             pltpu.make_async_copy(ids_in, meta.at[pl.ds(0, 8)], load_sem.at[2]),
             pltpu.make_async_copy(scores_in, meta.at[pl.ds(8, 8)], load_sem.at[3])]
    for i, ref in enumerate((wg, wu, wd)):
        loads.append(pltpu.make_async_copy(ref, weights.at[i, rows_of(part)], load_sem.at[4 + i]))
    for load in loads:
        load.start()
    spread[...] = one_hot(lax.broadcasted_iota(jnp.int32, (ROWS, EXPERTS), 0) // 8
                          == lax.broadcasted_iota(jnp.int32, (ROWS, EXPERTS), 1)).astype(BF16)
    acc[...] = jnp.zeros_like(acc)
    for load in loads:
        load.wait()
    pl.semaphore_wait(entry, 49)

    remote(grad, gath_g.at[2], gath_send, gath_recv.at[2], z_back).start()
    remote(grad, gath_g.at[1], gath_send, gath_recv.at[1], z_near).start()
    remote(tok, ring_t.at[1], ring_send, ring_recv.at[1], y_next).start()
    remote(tok, ring_t.at[7], ring_send, ring_recv.at[7], y_prev).start()
    for j, target in ((2, z_back), (1, z_near), (3, z_far)):
        remote(meta, gath_m.at[j], id_send.at[0], id_recv.at[0], target).start()

    def send_ids(dy, carry):
        target = device_at(x, lax.rem(y + dy, 8), z_pair, z_low, core)
        remote(meta.at[pl.ds(0, 8)], ring_i.at[dy], id_send.at[1], id_recv.at[1], target).start()
        return carry

    lax.fori_loop(1, 8, send_ids, 0)
    remote(own_weights, own_weights, w_send, w_recv.at[0], other_chip).start()
    remote(own_weights, own_weights, w_send, w_recv.at[1], other_core).start()

    def send_tokens(dy):
        block = tok if dy == 0 else ring_t.at[dy]
        chunk, side = place_of(dy)
        rows = pl.ds(dy * TOK, TOK)
        send_t[rows] = dot(pick_y[rows], block[...], ((1,), (0,))).astype(BF16)

        def one(index, carry):
            j, dx = lax.rem(index, 4), index // 4
            dz = jnp.where(j == 0, 0, jnp.where(j == 3, 2, jnp.where(j == 1, dz_near, dz_back)))
            z_low_to = jnp.where(j < 2, z_low, 1 - z_low)
            x_to, z_to = lax.rem(x + dx, 4), lax.rem(z_pair + dz, 4)
            src = pl.ds(pl.multiple_of(dy * TOK + (z_to * 4 + x_to) * 8, 8), 8)
            dst = pl.ds(pl.multiple_of(slot_of(chunk, side, dx, j) * 8, 8), 8)

            @pl.when(index == 0)
            def _():
                pltpu.make_async_copy(send_t.at[src], recv_t.at[dst], recv_t_sem.at[chunk]).start()

            @pl.when(index > 0)
            def _():
                target = device_at(x_to, y, z_to, z_low_to, core)
                remote(send_t.at[src], recv_t.at[dst], send_sem.at[0], recv_t_sem.at[chunk], target).start()

            return carry

        lax.fori_loop(0, 16, one, 0)

    def send_grads(j):
        block = grad if j == 0 else gath_g.at[j]
        rows = pl.ds(j * 256, 256)
        send_g[rows] = dot(gated_z[rows], block[...], ((1,), (0,))).astype(BF16)

        def one(index, carry):
            chunk, side, dx = index // 8, lax.rem(index, 2), lax.rem(index // 2, 4)
            dy = dy_of(chunk, side)
            x_to, y_to = lax.rem(x + dx, 4), lax.rem(y + dy, 8)
            src = pl.ds(pl.multiple_of(j * 256 + (y_to * 4 + x_to) * 8, 8), 8)
            dst = pl.ds(pl.multiple_of(slot_of(chunk, side, dx, j) * 8, 8), 8)
            here = (dx + dy) == 0

            @pl.when(here)
            def _():
                pltpu.make_async_copy(send_g.at[src], recv_g.at[dst], recv_g_sem.at[chunk]).start()

            @pl.when(jnp.logical_not(here))
            def _():
                target = device_at(x_to, y_to, z_pair, z_low, core)
                remote(send_g.at[src], recv_g.at[dst], send_sem.at[1], recv_g_sem.at[chunk], target).start()

            return carry

        lax.fori_loop(0, 32, one, 0)

    def wait_ring(dy):
        pltpu.make_async_copy(ring_t.at[dy], ring_t.at[dy], ring_recv.at[dy]).wait()

    def pass_on(dy, to, target, rows=None):
        src, dst = ring_t.at[dy], ring_t.at[to]
        if rows is not None:
            src, dst = src.at[rows], dst.at[rows]
        remote(src, dst, ring_send, ring_recv.at[to], target).start()

    def wait_gath(j):
        pltpu.make_async_copy(gath_g.at[j], gath_g.at[j], gath_recv.at[j]).wait()

    metas = gath_m.at[pl.ds(1, 3)]
    pltpu.make_async_copy(metas, metas, id_recv.at[0]).wait()
    all_ids = ring_i.at[pl.ds(1, 7)]
    pltpu.make_async_copy(all_ids, all_ids, id_recv.at[1]).wait()
    pick_z[...], gated_z[...] = routing([meta[0:8]] + [gath_m[j, 0:8] for j in range(1, 4)],
                                        lambda e: (e // 4) * 16 + z_pair * 4 + lax.rem(e, 4),
                                        [meta[8:16]] + [gath_m[j, 8:16] for j in range(1, 4)], spread[...])
    send_grads(0)
    wait_ring(1)
    pass_on(1, 2, y_next)
    wait_ring(7)
    pass_on(7, 6, y_prev)
    wait_gath(2)
    remote(gath_g.at[2], gath_g.at[3], gath_send, gath_recv.at[3], z_near).start()
    pick_y[...], _ = routing([meta[0:8]] + [ring_i[dy] for dy in range(1, 8)], lambda e: y * 16 + e, None, spread[...])
    send_grads(2)
    send_tokens(1)
    send_tokens(7)
    w_chip = weights.at[:, rows_of(part_chip)]
    pltpu.make_async_copy(w_chip, w_chip, w_recv.at[0]).wait()
    remote(w_chip, w_chip, w_send, w_recv.at[2], other_core).start()
    wait_ring(2)
    pass_on(2, 3, y_next)
    wait_ring(6)
    pass_on(6, 5, y_prev)
    wait_gath(1)
    send_grads(1)
    send_tokens(2)
    send_tokens(6)
    wait_gath(3)
    send_grads(3)
    wait_ring(3)
    pass_on(3, 4, y_next, pl.ds(0, TOK // 2))
    wait_ring(5)
    pass_on(5, 4, y_prev, pl.ds(TOK // 2, TOK // 2))
    send_tokens(3)
    send_tokens(5)
    send_tokens(0)
    wait_ring(4)
    send_tokens(4)
    w_core = weights.at[:, rows_of(part_core)]
    w_far = weights.at[:, rows_of(part_far)]
    pltpu.make_async_copy(w_core, w_core, w_recv.at[1]).wait()
    pltpu.make_async_copy(w_far, w_far, w_recv.at[2]).wait()

    def compute(c):
        rows = pl.ds(c * CHUNK, CHUNK)
        pltpu.make_async_copy(recv_t.at[rows], recv_t.at[rows], recv_t_sem.at[c]).wait()
        pltpu.make_async_copy(recv_g.at[rows], recv_g.at[rows], recv_g_sem.at[c]).wait()
        row_in = recv_t[rows]
        scaled = recv_g[rows]
        a = dot(row_in, weights[0], ((1,), (0,)))
        b = dot(row_in, weights[1], ((1,), (0,)))
        back = dot(scaled, weights[2], ((1,), (0,)))
        sig = jax.nn.sigmoid(a)
        silu = a * sig
        hidden = (silu * b).astype(BF16)
        gate_back = (back * b * sig * (1.0 + a * (1.0 - sig))).astype(BF16)
        up_back = (back * silu).astype(BF16)
        token_part = (dot(gate_back, weights[0], ((1,), (1,)))
                      + dot(up_back, weights[1], ((1,), (1,)))).astype(BF16)
        part_y[rows] = token_part[:, :D // 2]
        part_z[rows] = token_part[:, D // 2:]

        def give_back(index, carry):
            side, j, dx = lax.rem(index, 2), lax.rem(index // 2, 4), index // 8
            dy = dy_of(c, side)
            dz = jnp.where(j == 0, 0, jnp.where(j == 3, 2, dz_near))
            z_low_from = jnp.where(j < 2, z_low, 1 - z_low)
            x_to, y_to, z_to = lax.rem(x + 4 - dx, 4), lax.rem(y + 8 - dy, 8), lax.rem(z_pair + 4 - dz, 4)
            src = pl.ds(pl.multiple_of(slot_of(c, side, dx, j) * 8, 8), 8)
            dst_y = ret_y.at[dy, pl.ds(pl.multiple_of((z_pair * 4 + x) * 8, 8), 8)]
            dst_z = ret_z.at[j, pl.ds(pl.multiple_of((y * 4 + x) * 8, 8), 8)]
            stays_y = (dx + j) == 0
            stays_z = (dx + dy) == 0

            @pl.when(stays_z)
            def _():
                pltpu.make_async_copy(part_z.at[src], dst_z, ret_z_sem.at[j]).start()

            @pl.when(jnp.logical_not(stays_z))
            def _():
                target = device_at(x_to, y_to, z_pair, z_low, core)
                remote(part_z.at[src], dst_z, ret_send.at[1], ret_z_sem.at[j], target).start()

            @pl.when(stays_y)
            def _():
                pltpu.make_async_copy(part_y.at[src], dst_y, ret_y_sem.at[dy]).start()

            @pl.when(jnp.logical_not(stays_y))
            def _():
                target = device_at(x_to, y, z_to, z_low_from, core)
                remote(part_y.at[src], dst_y, ret_send.at[0], ret_y_sem.at[dy], target).start()

            return carry

        lax.fori_loop(0, 32, give_back, 0)
        acc[0] += dot(row_in, gate_back, ((0,), (0,)))
        acc[1] += dot(row_in, up_back, ((0,), (0,)))
        acc[2] += dot(scaled, hidden, ((0,), (0,)))

    def per_token_y(dy):
        pltpu.make_async_copy(ret_y.at[dy], ret_y.at[dy], ret_y_sem.at[dy]).wait()
        return dot(pick_y[pl.ds(dy * TOK, TOK)], ret_y[dy], ((0,), (0,)))

    def per_token_z(j):
        pltpu.make_async_copy(ret_z.at[j], ret_z.at[j], ret_z_sem.at[j]).wait()
        return dot(pick_z[pl.ds(j * 256, 256)], ret_z[j], ((0,), (0,)))

    low, high = pl.ds(0, TOK // 2), pl.ds(TOK // 2, TOK // 2)

    def wait_got_y(slot, rows=None):
        ref = got_y.at[slot] if rows is None else got_y.at[slot, rows]
        pltpu.make_async_copy(ref, ref, got_y_sem.at[slot]).wait()

    def start_sum_y():
        sum_y[4] = per_token_y(4).astype(BF16)
        remote(sum_y.at[4, low], got_y.at[3, low], sum_send.at[0], got_y_sem.at[3], y_prev).start()
        remote(sum_y.at[4, high], got_y.at[5, high], sum_send.at[0], got_y_sem.at[5], y_next).start()

    def step_sum_y(dy, to, target):
        total = per_token_y(dy)
        if dy == 3:
            wait_got_y(3, low)
            half = TOK // 2
            sum_y[3, 0:half] = (total[0:half] + got_y[3, 0:half].astype(F32)).astype(BF16)
            sum_y[3, half:TOK] = total[half:TOK].astype(BF16)
        elif dy == 5:
            wait_got_y(5, high)
            half = TOK // 2
            sum_y[5, 0:half] = total[0:half].astype(BF16)
            sum_y[5, half:TOK] = (total[half:TOK] + got_y[5, half:TOK].astype(F32)).astype(BF16)
        else:
            wait_got_y(dy)
            sum_y[dy] = (total + got_y[dy].astype(F32)).astype(BF16)
        remote(sum_y.at[dy], got_y.at[to], sum_send.at[0], got_y_sem.at[to], target).start()

    compute(0)
    compute(1)
    start_sum_y()
    compute(2)
    step_sum_y(3, 2, y_prev)
    step_sum_y(5, 6, y_next)
    compute(3)
    for i in range(3):
        for zl in range(2):
            half_s[i, zl] = acc[i, rows_of(zl * 2 + 1 - core)].astype(BF16)
    half = remote(half_s, half_r, red_send.at[0], red_recv.at[0], other_core)
    half.start()
    step_sum_y(2, 1, y_prev)
    step_sum_y(6, 7, y_next)
    half.wait()
    for i in range(3):
        quarter_s[i] = (acc[i, rows_of(part_chip)] + half_r[i, 1 - z_low].astype(F32)).astype(BF16)
    quarter = remote(quarter_s, quarter_r, red_send.at[1], red_recv.at[1], other_chip)
    quarter.start()
    sum_z[3] = per_token_z(3).astype(BF16)
    remote(sum_z.at[3], got_z.at[3], sum_send.at[1], got_z_sem.at[3], z_from).start()
    step_sum_y(1, 0, y_prev)
    step_sum_y(7, 4, y_next)
    sum_z[1] = per_token_z(1).astype(BF16)
    remote(sum_z.at[1], got_z.at[1], sum_send.at[1], got_z_sem.at[1], z_from).start()
    own_z2 = per_token_z(2)
    pltpu.make_async_copy(got_z.at[3], got_z.at[3], got_z_sem.at[3]).wait()
    sum_z[2] = (own_z2 + got_z[3].astype(F32)).astype(BF16)
    remote(sum_z.at[2], got_z.at[2], sum_send.at[1], got_z_sem.at[2], z_back).start()
    own_y = per_token_y(0)
    own_z = per_token_z(0)
    wait_got_y(0)
    wait_got_y(4)
    d_tok[:, 0:D // 2] = (own_y + got_y[0].astype(F32) + got_y[4].astype(F32)).astype(BF16)
    quarter.wait()
    outs = (g_gate, g_up, g_down)
    for i in range(3):
        outs[i][...] = acc[i, rows_of(part)] + half_r[i, z_low].astype(F32) + quarter_r[i].astype(F32)
    pltpu.make_async_copy(got_z.at[1], got_z.at[1], got_z_sem.at[1]).wait()
    pltpu.make_async_copy(got_z.at[2], got_z.at[2], got_z_sem.at[2]).wait()
    d_tok[:, D // 2:D] = (own_z + got_z[1].astype(F32) + got_z[2].astype(F32)).astype(BF16)

    def wait_sent(ref, sem):
        pltpu.make_async_copy(ref, ref, sem).wait()

    wait_sent(send_t.at[pl.ds(0, ROWS - 64)], send_sem.at[0])
    wait_sent(send_g.at[pl.ds(0, ROWS - 32)], send_sem.at[1])
    wait_sent(part_y.at[pl.ds(0, ROWS - 64)], ret_send.at[0])
    wait_sent(part_z.at[pl.ds(0, ROWS - 32)], ret_send.at[1])
    wait_sent(ring_t.at[pl.ds(1, 7)], ring_send)
    wait_sent(gath_g.at[pl.ds(1, 3)], gath_send)
    wait_sent(metas, id_send.at[0])
    wait_sent(all_ids, id_send.at[1])
    wait_sent(sum_y.at[pl.ds(1, 7)], sum_send.at[0])
    wait_sent(sum_z.at[pl.ds(1, 3)], sum_send.at[1])
    for _ in range(3):
        wait_sent(w_chip, w_send)


def per_device(tokens, out_grad, expert_ids, gate_scores, w_gate, w_up, w_down):
    vmem = pl.BlockSpec(memory_space=pltpu.VMEM)
    block = jax.ShapeDtypeStruct((DQ, HID), F32)
    dma = pltpu.SemaphoreType.DMA
    half = D // 2
    d_tokens, gate, up, down = pl.pallas_call(
        body,
        out_shape=(jax.ShapeDtypeStruct((TOK, D), BF16), block, block, block),
        in_specs=[pl.BlockSpec(memory_space=pl.ANY)] * 7,
        out_specs=(vmem,) * 4,
        scratch_shapes=[
            pltpu.VMEM((TOK, D), BF16),
            pltpu.VMEM((TOK, D), BF16),
            pltpu.VMEM((16, TOK), jnp.int32),
            pltpu.VMEM((ROWS, EXPERTS), BF16),
            pltpu.VMEM((ROWS, TOK), BF16),
            pltpu.VMEM((ROWS, TOK), BF16),
            pltpu.VMEM((ROWS, TOK), BF16),
            pltpu.VMEM((8, TOK, D), BF16),
            pltpu.VMEM((8, 8, TOK), jnp.int32),
            pltpu.VMEM((4, TOK, D), BF16),
            pltpu.VMEM((4, 16, TOK), jnp.int32),
            pltpu.VMEM((ROWS, D), BF16),
            pltpu.VMEM((ROWS, D), BF16),
            pltpu.VMEM((ROWS, D), BF16),
            pltpu.VMEM((ROWS, D), BF16),
            pltpu.VMEM((ROWS, half), BF16),
            pltpu.VMEM((ROWS, half), BF16),
            pltpu.VMEM((8, TOK, half), BF16),
            pltpu.VMEM((4, 256, half), BF16),
            pltpu.VMEM((8, TOK, half), BF16),
            pltpu.VMEM((4, TOK, half), BF16),
            pltpu.VMEM((8, TOK, half), BF16),
            pltpu.VMEM((4, TOK, half), BF16),
            pltpu.VMEM((3, D, HID), BF16),
            pltpu.VMEM((3, D, HID), F32),
            pltpu.VMEM((3, 2, DQ, HID), BF16),
            pltpu.VMEM((3, 2, DQ, HID), BF16),
            pltpu.VMEM((3, DQ, HID), BF16),
            pltpu.VMEM((3, DQ, HID), BF16),
            dma((7,)),
            dma,
            dma((8,)),
            dma,
            dma((4,)),
            dma((2,)),
            dma((2,)),
            dma((2,)),
            dma((CHUNKS,)),
            dma((CHUNKS,)),
            dma,
            dma((3,)),
            dma((2,)),
            dma((8,)),
            dma((4,)),
            dma((2,)),
            dma((8,)),
            dma((4,)),
            dma((2,)),
            dma((2,)),
        ],
        compiler_params=pltpu.CompilerParams(
            collective_id=0, has_side_effects=True, vmem_limit_bytes=56 << 20),
        name="expert_layer_backward",
    )(tokens, out_grad, expert_ids.T, gate_scores.T, w_gate[0], w_up[0], w_down[0])
    return d_tokens, gate[None], up[None], down[None]


def solution(mesh):
    rows = P(("expert", "dp"), None)
    blocks = P(("expert", "dp"), None, None)
    return jax.shard_map(
        per_device,
        mesh=mesh,
        in_specs=(rows, rows, rows, rows, blocks, blocks, blocks),
        out_specs=(rows, blocks, blocks, blocks),
        check_vma=False,
    )
```

time: 463 us -> 159 us (0.34)
  the two profiles are of different devices: /device:TPU:24 before, /device:TPU:1 now
where the time goes in v1:
time: 159 us
  Pallas kernels  154 us (97%)
  local copies, waits for them, and re-layouts  4.74 us (3%)
    pallas_call x1, Pallas kernels, per_device(): pl.pallas_call(body, out_shape=(jax.ShapeDtypeStruct((TOK, D), BF16), blo...  154 us
    unnamed x10, local copies, waits for them, and re-layouts  4.74 us

profile of v1, /device:TPU:1, one launch (start us, length us, event | category | flops | bytes accessed | tf_op | source)
XLA Modules:
  0.0 159.0 jit_solution(13835277680786027716)
XLA Ops:
  0.6 153.6 %expert_layer_backward.1 = (bf16[128,1024]{1,0:T(8,128)(2,1)}, f32[256,384]{1,0:T(8,128)}, f32[256,384]{1,0:T(8,128)}, f32[256,384]{1,0:T(8,128)}) custom-call(bf16[128,1024]{1,0:T(8,128)(2,1)} %tok_in.1, bf16[128,1024]{1,0:T(8,128)(2,1)} %grad_in.1, s32[8,128]{1,0:T(8,128)} %bitcast.14, s32[8,128]{1,0:T(8,128)} %bitcast.15, bf16[256,384]{1,0:T(8,128)(2,1)} %bitcast.11, ...), custom_call_target="tpu_custom_call" | custom-call | tf_op jit(solution)/shard_map/expert_layer_backward/pallas_call | solution.py:433
  154.3 0.0 copy-start.2
  154.3 1.7 %copy.15 = bf16[128,1024]{1,0:T(8,128)(2,1)} copy(bf16[128,1024]{1,0:T(8,128)(2,1)} %get-tuple-element.16) | data formatting | bytes 524288
  156.0 0.0 copy-done.2
  156.0 0.0 copy-start.1
  156.0 0.7 copy.16
  156.8 0.4 copy-done.1
  157.2 0.0 copy-start
  157.2 0.7 copy.17
  157.9 0.4 copy-done
  158.3 0.7 copy.18
Async XLA Ops:
  154.3 1.7 %copy-start.2 = (f32[256,384]{1,0:T(8,128)S(1)}, f32[256,384]{1,0:T(8,128)}, u32[]{:S(2)}) copy-start(f32[256,384]{1,0:T(8,128)} %get-tuple-element.9) | copy-start | bytes 1179652
  156.0 1.1 copy-start.1
  157.2 1.1 copy-start

commit v2 on v1

--- a/solution.py
+++ b/solution.py
@@ -12,6 +12,7 @@
 EXPERTS = 128
 ROWS = 1024
 CHUNKS = 4
+SUB = 2
 CHUNK = ROWS // CHUNKS
 DQ = 256
 F32 = jnp.float32
@@ -150,8 +151,10 @@
 
     remote(grad, gath_g.at[2], gath_send, gath_recv.at[2], z_back).start()
     remote(grad, gath_g.at[1], gath_send, gath_recv.at[1], z_near).start()
-    remote(tok, ring_t.at[1], ring_send, ring_recv.at[1], y_next).start()
-    remote(tok, ring_t.at[7], ring_send, ring_recv.at[7], y_prev).start()
+    for n in range(SUB):
+        rows = pl.ds(n * (TOK // SUB), TOK // SUB)
+        remote(tok.at[rows], ring_t.at[1, rows], ring_send, ring_recv.at[1, n], y_next).start()
+        remote(tok.at[rows], ring_t.at[7, rows], ring_send, ring_recv.at[7, n], y_prev).start()
     for j, target in ((2, z_back), (1, z_near), (3, z_far)):
         remote(meta, gath_m.at[j], id_send.at[0], id_recv.at[0], target).start()
 
@@ -191,13 +194,14 @@
 
         lax.fori_loop(0, 16, one, 0)
 
-    def send_grads(j):
+    def scale_grads(j):
         block = grad if j == 0 else gath_g.at[j]
         rows = pl.ds(j * 256, 256)
         send_g[rows] = dot(gated_z[rows], block[...], ((1,), (0,))).astype(BF16)
 
+    def send_grads(chunk):
         def one(index, carry):
-            chunk, side, dx = index // 8, lax.rem(index, 2), lax.rem(index // 2, 4)
+            side, j, dx = lax.rem(index, 2), lax.rem(index // 2, 4), index // 8
             dy = dy_of(chunk, side)
             x_to, y_to = lax.rem(x + dx, 4), lax.rem(y + dy, 8)
             src = pl.ds(pl.multiple_of(j * 256 + (y_to * 4 + x_to) * 8, 8), 8)
@@ -217,14 +221,16 @@
 
         lax.fori_loop(0, 32, one, 0)
 
-    def wait_ring(dy):
-        pltpu.make_async_copy(ring_t.at[dy], ring_t.at[dy], ring_recv.at[dy]).wait()
-
-    def pass_on(dy, to, target, rows=None):
-        src, dst = ring_t.at[dy], ring_t.at[to]
-        if rows is not None:
-            src, dst = src.at[rows], dst.at[rows]
-        remote(src, dst, ring_send, ring_recv.at[to], target).start()
+    def ring_rows(n):
+        return pl.ds(n * (TOK // SUB), TOK // SUB)
+
+    def wait_ring(dy, n):
+        ref = ring_t.at[dy, ring_rows(n)]
+        pltpu.make_async_copy(ref, ref, ring_recv.at[dy, n]).wait()
+
+    def pass_on(dy, to, n, target):
+        remote(ring_t.at[dy, ring_rows(n)], ring_t.at[to, ring_rows(n)],
+               ring_send, ring_recv.at[to, n], target).start()
 
     def wait_gath(j):
         pltpu.make_async_copy(gath_g.at[j], gath_g.at[j], gath_recv.at[j]).wait()
@@ -236,43 +242,36 @@
     pick_z[...], gated_z[...] = routing([meta[0:8]] + [gath_m[j, 0:8] for j in range(1, 4)],
                                         lambda e: (e // 4) * 16 + z_pair * 4 + lax.rem(e, 4),
                                         [meta[8:16]] + [gath_m[j, 8:16] for j in range(1, 4)], spread[...])
-    send_grads(0)
-    wait_ring(1)
-    pass_on(1, 2, y_next)
-    wait_ring(7)
-    pass_on(7, 6, y_prev)
-    wait_gath(2)
-    remote(gath_g.at[2], gath_g.at[3], gath_send, gath_recv.at[3], z_near).start()
-    pick_y[...], _ = routing([meta[0:8]] + [ring_i[dy] for dy in range(1, 8)], lambda e: y * 16 + e, None, spread[...])
-    send_grads(2)
-    send_tokens(1)
-    send_tokens(7)
+    def make_pick_y():
+        pick_y[...], _ = routing([meta[0:8]] + [ring_i[dy] for dy in range(1, 8)], lambda e: y * 16 + e, None, spread[...])
+
+    def hops(step):
+        for n in range(SUB):
+            wait_ring(step, n)
+            if step < 3 or n < SUB // 2:
+                pass_on(step, step + 1, n, y_next)
+            wait_ring(8 - step, n)
+            if step < 3 or n >= SUB // 2:
+                pass_on(8 - step, 7 - step, n, y_prev)
+
+    def relay():
+        wait_gath(2)
+        remote(gath_g.at[2], gath_g.at[3], gath_send, gath_recv.at[3], z_near).start()
+
     w_chip = weights.at[:, rows_of(part_chip)]
-    pltpu.make_async_copy(w_chip, w_chip, w_recv.at[0]).wait()
-    remote(w_chip, w_chip, w_send, w_recv.at[2], other_core).start()
-    wait_ring(2)
-    pass_on(2, 3, y_next)
-    wait_ring(6)
-    pass_on(6, 5, y_prev)
-    wait_gath(1)
-    send_grads(1)
-    send_tokens(2)
-    send_tokens(6)
-    wait_gath(3)
-    send_grads(3)
-    wait_ring(3)
-    pass_on(3, 4, y_next, pl.ds(0, TOK // 2))
-    wait_ring(5)
-    pass_on(5, 4, y_prev, pl.ds(TOK // 2, TOK // 2))
-    send_tokens(3)
-    send_tokens(5)
-    send_tokens(0)
-    wait_ring(4)
-    send_tokens(4)
-    w_core = weights.at[:, rows_of(part_core)]
-    w_far = weights.at[:, rows_of(part_far)]
-    pltpu.make_async_copy(w_core, w_core, w_recv.at[1]).wait()
-    pltpu.make_async_copy(w_far, w_far, w_recv.at[2]).wait()
+
+    def pass_weights():
+        pltpu.make_async_copy(w_chip, w_chip, w_recv.at[0]).wait()
+        remote(w_chip, w_chip, w_send, w_recv.at[2], other_core).start()
+
+    def last_block():
+        for n in range(SUB):
+            wait_ring(4, n)
+
+    def wait_weights():
+        for n, p in ((1, part_core), (2, part_far)):
+            ref = weights.at[:, rows_of(p)]
+            pltpu.make_async_copy(ref, ref, w_recv.at[n]).wait()
 
     def compute(c):
         rows = pl.ds(c * CHUNK, CHUNK)
@@ -328,7 +327,12 @@
         lax.fori_loop(0, 32, give_back, 0)
         acc[0] += dot(row_in, gate_back, ((0,), (0,)))
         acc[1] += dot(row_in, up_back, ((0,), (0,)))
+        if c == CHUNKS - 1:
+            start_half(0)
+            start_half(1)
         acc[2] += dot(scaled, hidden, ((0,), (0,)))
+        if c == CHUNKS - 1:
+            start_half(2)
 
     def per_token_y(dy):
         pltpu.make_async_copy(ret_y.at[dy], ret_y.at[dy], ret_y_sem.at[dy]).wait()
@@ -366,25 +370,60 @@
             sum_y[dy] = (total + got_y[dy].astype(F32)).astype(BF16)
         remote(sum_y.at[dy], got_y.at[to], sum_send.at[0], got_y_sem.at[to], target).start()
 
+    def half(i):
+        return remote(half_s.at[i], half_r.at[i], red_send.at[i], red_recv.at[i], other_core)
+
+    def quarter(i):
+        return remote(quarter_s.at[i], quarter_r.at[i], red_send.at[3 + i], red_recv.at[3 + i], other_chip)
+
+    def start_half(i):
+        for zl in range(2):
+            half_s[i, zl] = acc[i, rows_of(zl * 2 + 1 - core)].astype(BF16)
+        half(i).start()
+
+    def wait_half(i):
+        half(i).wait()
+
+    hops(1)
+    relay()
+    make_pick_y()
+    send_tokens(0)
+    scale_grads(0)
+    hops(2)
+    scale_grads(2)
+    send_tokens(1)
+    send_tokens(7)
+    pass_weights()
+    wait_gath(1)
+    scale_grads(1)
+    hops(3)
+    wait_gath(3)
+    scale_grads(3)
+    send_grads(0)
+    send_tokens(3)
+    send_tokens(5)
+    last_block()
+    send_tokens(4)
+    send_grads(1)
+    send_tokens(2)
+    send_tokens(6)
+    send_grads(2)
+    wait_weights()
     compute(0)
+    send_grads(3)
     compute(1)
     start_sum_y()
     compute(2)
     step_sum_y(3, 2, y_prev)
     step_sum_y(5, 6, y_next)
     compute(3)
-    for i in range(3):
-        for zl in range(2):
-            half_s[i, zl] = acc[i, rows_of(zl * 2 + 1 - core)].astype(BF16)
-    half = remote(half_s, half_r, red_send.at[0], red_recv.at[0], other_core)
-    half.start()
     step_sum_y(2, 1, y_prev)
     step_sum_y(6, 7, y_next)
-    half.wait()
+    for i in range(3):
+        wait_half(i)
     for i in range(3):
         quarter_s[i] = (acc[i, rows_of(part_chip)] + half_r[i, 1 - z_low].astype(F32)).astype(BF16)
-    quarter = remote(quarter_s, quarter_r, red_send.at[1], red_recv.at[1], other_chip)
-    quarter.start()
+        quarter(i).start()
     sum_z[3] = per_token_z(3).astype(BF16)
     remote(sum_z.at[3], got_z.at[3], sum_send.at[1], got_z_sem.at[3], z_from).start()
     step_sum_y(1, 0, y_prev)
@@ -400,7 +439,8 @@
     wait_got_y(0)
     wait_got_y(4)
     d_tok[:, 0:D // 2] = (own_y + got_y[0].astype(F32) + got_y[4].astype(F32)).astype(BF16)
-    quarter.wait()
+    for i in range(3):
+        quarter(i).wait()
     outs = (g_gate, g_up, g_down)
     for i in range(3):
         outs[i][...] = acc[i, rows_of(part)] + half_r[i, z_low].astype(F32) + quarter_r[i].astype(F32)
@@ -467,7 +507,7 @@
             pltpu.VMEM((3, DQ, HID), BF16),
             dma((7,)),
             dma,
-            dma((8,)),
+            dma((8, SUB)),
             dma,
             dma((4,)),
             dma((2,)),
@@ -483,11 +523,11 @@
             dma((2,)),
             dma((8,)),
             dma((4,)),
-            dma((2,)),
-            dma((2,)),
+            dma((6,)),
+            dma((6,)),
         ],
         compiler_params=pltpu.CompilerParams(
-            collective_id=0, has_side_effects=True, vmem_limit_bytes=56 << 20),
+            collective_id=0, has_side_effects=True, vmem_limit_bytes=40 << 20),
         name="expert_layer_backward",
     )(tokens, out_grad, expert_ids.T, gate_scores.T, w_gate[0], w_up[0], w_down[0])
     return d_tokens, gate[None], up[None], down[None]

time: 159 us -> 150 us (0.943)
  Pallas kernels: 154 us -> 141 us
  local copies, waits for them, and re-layouts: 4.74 us -> 8.31 us
    pallas_call x1, Pallas kernels: 154 us -> 141 us  [per_device(): pl.pallas_call(body, out_shape=(jax.ShapeDtypeStruct((TOK, D), BF16), blo...]
    unnamed x10 -> x18, local copies, waits for them, and re-layouts: 4.74 us -> 8.31 us
where the time goes in v2:
time: 150 us
  Pallas kernels  141 us (94%)
  local copies, waits for them, and re-layouts  8.31 us (6%)
    pallas_call x1, Pallas kernels, per_device(): pl.pallas_call(body, out_shape=(jax.ShapeDtypeStruct((TOK, D), BF16), blo...  141 us
    unnamed x18, local copies, waits for them, and re-layouts  8.31 us

profile of v2, /device:TPU:1, one launch (start us, length us, event | category | flops | bytes accessed | tf_op | source)
XLA Modules:
  0.0 149.5 jit_solution(2115580139807419877)
XLA Ops:
  0.6 0.0 copy-start.6
  0.6 0.0 copy-start.5
  0.7 0.7 copy-done.6
  1.3 0.0 copy-done.5
  1.3 0.0 copy-start
  1.3 0.9 copy-done
  2.3 0.0 copy-start.1
  2.3 0.9 copy-done.1
  3.2 0.0 copy-start.2
  3.2 0.9 copy-done.2
  4.2 0.0 copy-start.3
  4.2 0.9 copy-done.3
  5.1 0.0 copy-start.4
  5.1 0.9 copy-done.4
  6.0 140.6 %expert_layer_backward.1 = (bf16[128,1024]{1,0:T(8,128)(2,1)S(1)}, f32[256,384]{1,0:T(8,128)S(1)}, f32[256,384]{1,0:T(8,128)S(1)}, f32[256,384]{1,0:T(8,128)S(1)}) custom-call(bf16[128,1024]{1,0:T(8,128)(2,1)S(1)} %copy-done, bf16[128,1024]{1,0:T(8,128)(2,1)S(1)} %copy-done.1, s32[8,128]{1,0:T(8,128)S(1)} %bitcast.14, s32[8,128]{1,0:T(8,128)S(1)} %bitcast.15, ...), custom_call_target="tpu_custom_call" | custom-call | tf_op jit(solution)/shard_map/expert_layer_backward/pallas_call | solution.py:473
  146.6 0.7 copy.15
  147.3 0.7 copy.16
  148.1 0.7 copy.17
  148.8 0.7 copy.18
Async XLA Ops:
  0.6 0.7 copy-start.6
  0.6 0.7 copy-start.5
  1.3 0.9 copy-start
  2.3 0.9 copy-start.1
  3.2 0.9 copy-start.2
  4.2 0.9 copy-start.3
  5.1 0.9 copy-start.4

commit v3 on v2

--- a/solution.py
+++ b/solution.py
@@ -13,6 +13,7 @@
 ROWS = 1024
 CHUNKS = 4
 SUB = 2
+CUT = 768
 CHUNK = ROWS // CHUNKS
 DQ = 256
 F32 = jnp.float32
@@ -289,8 +290,8 @@
         up_back = (back * silu).astype(BF16)
         token_part = (dot(gate_back, weights[0], ((1,), (1,)))
                       + dot(up_back, weights[1], ((1,), (1,)))).astype(BF16)
-        part_y[rows] = token_part[:, :D // 2]
-        part_z[rows] = token_part[:, D // 2:]
+        part_y[rows] = token_part[:, :CUT]
+        part_z[rows] = token_part[:, CUT:]
 
         def give_back(index, carry):
             side, j, dx = lax.rem(index, 2), lax.rem(index // 2, 4), index // 8
@@ -417,13 +418,12 @@
     step_sum_y(3, 2, y_prev)
     step_sum_y(5, 6, y_next)
     compute(3)
+    for i in range(3):
+        wait_half(i)
+        quarter_s[i] = (acc[i, rows_of(part_chip)] + half_r[i, 1 - z_low].astype(F32)).astype(BF16)
+        quarter(i).start()
     step_sum_y(2, 1, y_prev)
     step_sum_y(6, 7, y_next)
-    for i in range(3):
-        wait_half(i)
-    for i in range(3):
-        quarter_s[i] = (acc[i, rows_of(part_chip)] + half_r[i, 1 - z_low].astype(F32)).astype(BF16)
-        quarter(i).start()
     sum_z[3] = per_token_z(3).astype(BF16)
     remote(sum_z.at[3], got_z.at[3], sum_send.at[1], got_z_sem.at[3], z_from).start()
     step_sum_y(1, 0, y_prev)
@@ -438,7 +438,7 @@
     own_z = per_token_z(0)
     wait_got_y(0)
     wait_got_y(4)
-    d_tok[:, 0:D // 2] = (own_y + got_y[0].astype(F32) + got_y[4].astype(F32)).astype(BF16)
+    d_tok[:, 0:CUT] = (own_y + got_y[0].astype(F32) + got_y[4].astype(F32)).astype(BF16)
     for i in range(3):
         quarter(i).wait()
     outs = (g_gate, g_up, g_down)
@@ -446,7 +446,7 @@
         outs[i][...] = acc[i, rows_of(part)] + half_r[i, z_low].astype(F32) + quarter_r[i].astype(F32)
     pltpu.make_async_copy(got_z.at[1], got_z.at[1], got_z_sem.at[1]).wait()
     pltpu.make_async_copy(got_z.at[2], got_z.at[2], got_z_sem.at[2]).wait()
-    d_tok[:, D // 2:D] = (own_z + got_z[1].astype(F32) + got_z[2].astype(F32)).astype(BF16)
+    d_tok[:, CUT:D] = (own_z + got_z[1].astype(F32) + got_z[2].astype(F32)).astype(BF16)
 
     def wait_sent(ref, sem):
         pltpu.make_async_copy(ref, ref, sem).wait()
@@ -469,7 +469,8 @@
     vmem = pl.BlockSpec(memory_space=pltpu.VMEM)
     block = jax.ShapeDtypeStruct((DQ, HID), F32)
     dma = pltpu.SemaphoreType.DMA
-    half = D // 2
+    operands = [pltpu.with_memory_space_constraint(value, pltpu.HBM) for value in (
+        tokens, out_grad, expert_ids.T, gate_scores.T, w_gate[0], w_up[0], w_down[0])]
     d_tokens, gate, up, down = pl.pallas_call(
         body,
         out_shape=(jax.ShapeDtypeStruct((TOK, D), BF16), block, block, block),
@@ -491,14 +492,14 @@
             pltpu.VMEM((ROWS, D), BF16),
             pltpu.VMEM((ROWS, D), BF16),
             pltpu.VMEM((ROWS, D), BF16),
-            pltpu.VMEM((ROWS, half), BF16),
-            pltpu.VMEM((ROWS, half), BF16),
-            pltpu.VMEM((8, TOK, half), BF16),
-            pltpu.VMEM((4, 256, half), BF16),
-            pltpu.VMEM((8, TOK, half), BF16),
-            pltpu.VMEM((4, TOK, half), BF16),
-            pltpu.VMEM((8, TOK, half), BF16),
-            pltpu.VMEM((4, TOK, half), BF16),
+            pltpu.VMEM((ROWS, CUT), BF16),
+            pltpu.VMEM((ROWS, D - CUT), BF16),
+            pltpu.VMEM((8, TOK, CUT), BF16),
+            pltpu.VMEM((4, 256, D - CUT), BF16),
+            pltpu.VMEM((8, TOK, CUT), BF16),
+            pltpu.VMEM((4, TOK, D - CUT), BF16),
+            pltpu.VMEM((8, TOK, CUT), BF16),
+            pltpu.VMEM((4, TOK, D - CUT), BF16),
             pltpu.VMEM((3, D, HID), BF16),
             pltpu.VMEM((3, D, HID), F32),
             pltpu.VMEM((3, 2, DQ, HID), BF16),
@@ -529,7 +530,7 @@
         compiler_params=pltpu.CompilerParams(
             collective_id=0, has_side_effects=True, vmem_limit_bytes=40 << 20),
         name="expert_layer_backward",
-    )(tokens, out_grad, expert_ids.T, gate_scores.T, w_gate[0], w_up[0], w_down[0])
+    )(*operands)
     return d_tokens, gate[None], up[None], down[None]
 
 

time: 150 us -> 141 us (0.940)
  the two profiles are of different devices: /device:TPU:1 before, /device:TPU:67 now
where the time goes in v3:
time: 141 us
  Pallas kernels  137 us (97%)
  local copies, waits for them, and re-layouts  2.94 us (2%)
    pallas_call x1, Pallas kernels, per_device(): pl.pallas_call(body, out_shape=(jax.ShapeDtypeStruct((TOK, D), BF16), blo...  137 us
    unnamed x4, local copies, waits for them, and re-layouts  2.94 us

profile of v3, /device:TPU:67, one launch (start us, length us, event | category | flops | bytes accessed | tf_op | source)
XLA Modules:
  0.0 140.9 jit_solution(4305421225365783150)
XLA Ops:
  0.6 137.3 %expert_layer_backward.1 = (bf16[128,1024]{1,0:T(8,128)(2,1)S(1)}, f32[256,384]{1,0:T(8,128)S(1)}, f32[256,384]{1,0:T(8,128)S(1)}, f32[256,384]{1,0:T(8,128)S(1)}) custom-call(bf16[128,1024]{1,0:T(8,128)(2,1)} %tok_in.1, bf16[128,1024]{1,0:T(8,128)(2,1)} %grad_in.1, s32[8,128]{1,0:T(8,128)} %bitcast.14, s32[8,128]{1,0:T(8,128)} %bitcast.15, ...), custom_call_target="tpu_custom_call" | custom-call | tf_op jit(solution)/shard_map/expert_layer_backward/pallas_call | solution.py:474
  137.9 0.7 copy.15
  138.6 0.7 copy.16
  139.4 0.7 copy.17
  140.1 0.7 copy.18

commit v4 on v3

--- a/solution.py
+++ b/solution.py
@@ -394,7 +394,6 @@
     scale_grads(2)
     send_tokens(1)
     send_tokens(7)
-    pass_weights()
     wait_gath(1)
     scale_grads(1)
     hops(3)
@@ -409,6 +408,7 @@
     send_tokens(2)
     send_tokens(6)
     send_grads(2)
+    pass_weights()
     wait_weights()
     compute(0)
     send_grads(3)

time: 141 us -> 141 us (level)
  the two profiles are of different devices: /device:TPU:67 before, /device:TPU:66 now
where the time goes in v4:
time: 141 us
  Pallas kernels  137 us (97%)
  local copies, waits for them, and re-layouts  2.94 us (2%)
    pallas_call x1, Pallas kernels, per_device(): pl.pallas_call(body, out_shape=(jax.ShapeDtypeStruct((TOK, D), BF16), blo...  137 us
    unnamed x4, local copies, waits for them, and re-layouts  2.94 us

profile of v4, /device:TPU:66, one launch (start us, length us, event | category | flops | bytes accessed | tf_op | source)
XLA Modules:
  0.0 140.9 jit_solution(17460993772904352718)
XLA Ops:
  0.6 137.3 %expert_layer_backward.1 = (bf16[128,1024]{1,0:T(8,128)(2,1)S(1)}, f32[256,384]{1,0:T(8,128)S(1)}, f32[256,384]{1,0:T(8,128)S(1)}, f32[256,384]{1,0:T(8,128)S(1)}) custom-call(bf16[128,1024]{1,0:T(8,128)(2,1)} %tok_in.1, bf16[128,1024]{1,0:T(8,128)(2,1)} %grad_in.1, s32[8,128]{1,0:T(8,128)} %bitcast.14, s32[8,128]{1,0:T(8,128)} %bitcast.15, ...), custom_call_target="tpu_custom_call" | custom-call | tf_op jit(solution)/shard_map/expert_layer_backward/pallas_call | solution.py:474
  137.9 0.7 copy.15
  138.6 0.7 copy.16
  139.4 0.7 copy.17
  140.1 0.7 copy.18
